TPU v7x, 128 devices: a whole 4x4x4 slice. The times are simulated.
128 devices in a mesh: dev: 128 (over x, z, y, core).
Axes of the slice: x: 4, y: 4, z: 4, core: 2. Of those that a mesh axis runs over, the one named last changes fastest.
Arguments:
- saved: bfloat16 [128, 1024, 768], P('dev'), may hold values from -6 to 6
- cotangent: bfloat16 [128, 1024, 2048], P('dev'), may hold values from -6 to 6
- weights: bfloat16 [128, 768, 2048], P('dev'), may hold values from -0.21875 to 0.21875
- counts: int32 [64], replicated, may hold values from 1 to 8, as said below
- live_rows: int32 [128], P('dev'), may hold values from 1 to 1024, 81920 in all
- next_map: int32 [128], replicated, may hold values from 0 to 63, as said below
- master: float32 [64, 768, 2048], P(None, 'dev'), may hold values from -0.21875 to 0.21875
- moment1: bfloat16 [64, 768, 2048], P(None, 'dev'), may hold values from -6 to 6
- moment2: bfloat16 [64, 768, 2048], P(None, 'dev'), may hold values from 0.049804688 to 4
Outputs:
- input_grads: bfloat16 [128, 1024, 768], P('dev')
- master_out: float32 [64, 768, 2048], P(None, 'dev')
- moment1_out: bfloat16 [64, 768, 2048], P(None, 'dev')
- moment2_out: bfloat16 [64, 768, 2048], P(None, 'dev')
- next_weights: bfloat16 [128, 768, 2048], P('dev')
Inputs may be any that keep to these rules, and one draw needn't show every extreme that they name: The counts sum to 128; in the current placement expert e holds the counts[e] slots that follow those of experts below e; some expert has exactly 8 replicas. `next_map`: every expert is named by 1 to 8 slots; some expert by exactly 8. `live_rows`: the live rows of all slots sum to 81920, and some slot has exactly 1024.
All inputs are finite; a program needn't handle non-finite values. No bound on the sum of `live_rows` on one device may be relied on, other than what follows from the above.
Results may differ from a plain program's by a relative error of at most 0.0058.
Values may be sent and summed in bfloat16 or wider, within the bound.
No kernel may reach another device: no remote copies, remote signals or barrier semaphores. Data moves between devices by JAX's collectives and lax.ppermute only.
A program may use at most 128 MiB of HBM per device.

v0:
```python
import functools
import jax
import jax.numpy as jnp
from jax import lax
from jax.experimental import pallas as pl
from jax.experimental.pallas import tpu as pltpu
from jax.sharding import PartitionSpec as P

LEARN_RATE = 0.001
DECAY_RATE = 0.1
BETA_ONE = 0.9
BETA_TWO = 0.95
BIAS_ONE = 1.0 - 0.9**20
BIAS_TWO = 1.0 - 0.95**20
EPSILON = 1e-08

LANES = 128
GROUP = 4


def contract_cols(left, right):
    return lax.dot_general(
        left, right, (((1,), (1,)), ((), ())), preferred_element_type=jnp.float32
    )


FAR = pl.BlockSpec(memory_space=pltpu.HBM)
NEAR = pl.BlockSpec(memory_space=pltpu.VMEM)
SCALARS = pl.BlockSpec(memory_space=pltpu.SMEM)


def grads_kernel(
    live_ref, saved_ref, cot_ref, out_ref,
    saved_in, cot_in, turned, sums, chunk, packed, saved_sem, cot_sem, out_sem,
):
    rows, hidden = saved_ref.shape
    steps, _, wide = cot_in.shape
    blocks = sums.shape[0]
    per_step = wide // LANES
    devices = out_ref.shape[0]
    share = hidden // devices
    tall = GROUP * share
    parts = out_sem.shape[0]
    part_size = devices // parts
    bands = saved_sem.shape[0]
    band_rows = rows // bands

    def load_saved(band):
        span = pl.ds(band * band_rows, band_rows)
        return pltpu.make_async_copy(saved_ref.at[span], saved_in.at[span], saved_sem.at[band])

    def load_cot(step):
        return pltpu.make_async_copy(
            cot_ref.at[:, step * wide : (step + 1) * wide], cot_in.at[step], cot_sem.at[step]
        )

    def send(part):
        span = pl.ds(part * part_size, part_size)
        return pltpu.make_async_copy(packed.at[span], out_ref.at[span], out_sem.at[part])

    for band in range(bands):
        load_saved(band).start()

    @pl.loop(0, bands)
    def _(band):
        span = pl.ds(pl.multiple_of(band * band_rows, band_rows), band_rows)
        pltpu.make_async_copy(saved_ref.at[span], saved_in.at[span], saved_sem.at[band]).wait()

        @pl.when(band == 0)
        def _():
            for step in range(steps):
                load_cot(step).start()

        index = lax.broadcasted_iota(jnp.int32, (band_rows, hidden), 0)
        part = saved_in[span, :]
        turned[:, span] = jnp.where(
            index < live_ref[0] - band * band_rows, part, jnp.zeros_like(part)
        ).T

    @pl.loop(0, steps)
    def _(step):
        pltpu.make_async_copy(cot_ref.at[:, :wide], cot_in.at[step], cot_sem.at[step]).wait()
        for start in range(0, wide, 2 * LANES):
            product = jnp.dot(
                turned[...],
                cot_in[step, :, start : start + 2 * LANES],
                preferred_element_type=jnp.float32,
            )
            for part in range(2):
                sums[step * per_step + start // LANES + part] = product[
                    :, part * LANES : (part + 1) * LANES
                ]

    for part in range(parts):

        @pl.loop(part * part_size // GROUP, (part + 1) * part_size // GROUP)
        def _(group):
            base = pl.multiple_of(group * tall, 8)
            for block in range(blocks):
                piece = sums[block, pl.ds(base, tall), :]
                for member in range(GROUP):
                    chunk[member, block * share : (block + 1) * share, :] = piece[
                        member * share : (member + 1) * share, :
                    ]
            for member in range(GROUP):
                packed[group * GROUP + member] = chunk[member].astype(jnp.bfloat16)

        send(part).start()
    for part in range(parts):
        send(part).wait()


def slot_chunks(saved, cot, live, devices, steps=4, parts=4, bands=4):
    rows, hidden = saved.shape
    width = cot.shape[1]
    wide = width // steps
    share = hidden // devices
    blocks = width // LANES
    return pl.pallas_call(
        grads_kernel,
        out_shape=jax.ShapeDtypeStruct((devices, blocks * share, LANES), jnp.bfloat16),
        in_specs=[SCALARS, FAR, FAR],
        out_specs=FAR,
        scratch_shapes=[
            pltpu.VMEM((rows, hidden), jnp.bfloat16),
            pltpu.VMEM((steps, rows, wide), jnp.bfloat16),
            pltpu.VMEM((hidden, rows), jnp.bfloat16),
            pltpu.VMEM((blocks, hidden, LANES), jnp.float32),
            pltpu.VMEM((GROUP, blocks * share, LANES), jnp.float32),
            pltpu.VMEM((devices, blocks * share, LANES), jnp.bfloat16),
            pltpu.SemaphoreType.DMA((bands,)),
            pltpu.SemaphoreType.DMA((steps,)),
            pltpu.SemaphoreType.DMA((parts,)),
        ],
        compiler_params=pltpu.CompilerParams(vmem_limit_bytes=63 << 20),
        cost_estimate=pl.CostEstimate(
            flops=2 * rows * hidden * width,
            bytes_accessed=2 * (rows * hidden + rows * width + hidden * width),
            transcendentals=0,
        ),
        name="slot_chunks",
    )(live, saved, cot)


def adam_kernel(
    holder_ref, fresh_ref, next_ref, pieces, master_ref, one_ref, two_ref,
    master_out, one_out, two_out, send_out,
    sums, master, one, two, outgoing, load_sem, store_sem, send_sem,
):
    slots, height, _ = pieces.shape
    share, experts, width = master_ref.shape
    blocks = width // LANES
    deep = 16
    tiles = experts // deep
    quad = GROUP * share
    arrays = ((master_ref, master, master_out), (one_ref, one, one_out), (two_ref, two, two_out))
    sends = send_sem.shape[0]
    send_size = slots // sends

    def loads(tile):
        span = pl.ds(pl.multiple_of(tile * deep, deep), deep)
        return [
            pltpu.make_async_copy(far.at[:, span, :], near.at[:, span, :], load_sem.at[which, tile])
            for which, (far, near, _) in enumerate(arrays)
        ]

    def stores(tile):
        span = pl.ds(pl.multiple_of(tile * deep, deep), deep)
        return [
            pltpu.make_async_copy(near.at[:, span, :], far.at[:, span, :], store_sem.at[which, tile])
            for which, (_, near, far) in enumerate(arrays)
        ]

    def send(part):
        span = pl.ds(part * send_size, send_size)
        return pltpu.make_async_copy(outgoing.at[span], send_out.at[span], send_sem.at[part])

    for tile in range(tiles):
        for copy in loads(tile):
            copy.start()

    def add_slot(slot, total):
        total = jnp.where(fresh_ref[slot] > 0, 0.0, total) + pieces[slot].astype(jnp.float32)
        sums[holder_ref[slot]] = total
        return total

    lax.fori_loop(0, slots, add_slot, jnp.zeros((height, LANES), jnp.float32), unroll=4)

    @pl.loop(0, tiles)
    def _(tile):
        for copy in loads(tile):
            copy.wait()
        rows = pl.ds(pl.multiple_of(tile * deep, deep), deep)

        @pl.loop(0, blocks // GROUP)
        def _(four):
            def place(half, band):
                return (
                    pl.ds(tile * deep + half * 8, 8),
                    pl.ds(pl.multiple_of(four * quad + band * 8, 8), 8),
                )

            for band in range(quad // 8):
                turned = [jnp.swapaxes(sums[place(half, band)], 0, 1) for half in range(2)]
                fresh = ([], [])
                for k in range(8):
                    block, row = divmod(band * 8 + k, share)
                    grad = jnp.concatenate([turned[0][k], turned[1][k]], axis=0)
                    lanes = pl.ds(pl.multiple_of((four * GROUP + block) * LANES, LANES), LANES)
                    first = (
                        BETA_ONE * one[row, rows, lanes].astype(jnp.float32)
                        + (1.0 - BETA_ONE) * grad
                    )
                    second = (
                        BETA_TWO * two[row, rows, lanes].astype(jnp.float32)
                        + (1.0 - BETA_TWO) * (grad * grad)
                    )
                    root = second * lax.rsqrt(second) * BIAS_TWO**-0.5 + EPSILON
                    new = (1.0 - LEARN_RATE * DECAY_RATE) * master[row, rows, lanes] - (
                        (LEARN_RATE / BIAS_ONE) * first
                    ) / root
                    master[row, rows, lanes] = new
                    one[row, rows, lanes] = first.astype(jnp.bfloat16)
                    two[row, rows, lanes] = second.astype(jnp.bfloat16)
                    fresh[0].append(new[:8])
                    fresh[1].append(new[8:])
                for half in range(2):
                    sums[place(half, band)] = jnp.swapaxes(jnp.stack(fresh[half]), 0, 1)

        for copy in stores(tile):
            copy.start()

    for part in range(sends):

        def fill(slot, carry):
            outgoing[slot] = sums[next_ref[slot]].astype(jnp.bfloat16)
            return carry

        lax.fori_loop(part * send_size, (part + 1) * send_size, fill, 0, unroll=4)
        send(part).start()

    for tile in range(tiles):
        for copy in stores(tile):
            copy.wait()
    for part in range(sends):
        send(part).wait()


def adam_step(holder, fresh, next_map, pieces, master, one, two, sends=4):
    slots, height, _ = pieces.shape
    share, experts, width = master.shape
    tiles = experts // 16
    return pl.pallas_call(
        adam_kernel,
        out_shape=(
            pltpu.HBM(master.shape, jnp.float32),
            pltpu.HBM(one.shape, jnp.bfloat16),
            pltpu.HBM(two.shape, jnp.bfloat16),
            pltpu.HBM((slots, height, LANES), jnp.bfloat16),
        ),
        in_specs=[SCALARS] * 3 + [NEAR] + [FAR] * 3,
        out_specs=(FAR,) * 4,
        scratch_shapes=[
            pltpu.VMEM((experts, height, LANES), jnp.float32),
            pltpu.VMEM(master.shape, jnp.float32),
            pltpu.VMEM(one.shape, jnp.bfloat16),
            pltpu.VMEM(two.shape, jnp.bfloat16),
            pltpu.VMEM(pieces.shape, jnp.bfloat16),
            pltpu.SemaphoreType.DMA((3, tiles)),
            pltpu.SemaphoreType.DMA((3, tiles)),
            pltpu.SemaphoreType.DMA((sends,)),
        ],
        compiler_params=pltpu.CompilerParams(vmem_limit_bytes=60 << 20),
        name="adam_step",
    )(
        holder, fresh, next_map, pltpu.with_memory_space_constraint(pieces, pltpu.VMEM),
        master, one, two,
    )


def rows_kernel(arrived, out_ref, wholes, chunk, tall, out_sem):
    slots, depth, _ = arrived.shape
    width = out_ref.shape[1]
    members = chunk.shape[0]
    blocks = width // LANES
    share = depth // blocks
    height = members * share
    parts = out_sem.shape[0]
    part_size = slots // parts

    def store(part):
        span = pl.ds(part * part_size * share, part_size * share)
        return pltpu.make_async_copy(wholes.at[span], out_ref.at[span], out_sem.at[part])

    for part in range(parts):

        @pl.loop(part * part_size // members, (part + 1) * part_size // members)
        def _(group):
            for member in range(members):
                chunk[member] = arrived[group * members + member].astype(jnp.float32)
            base = pl.multiple_of(group * height, 16)
            for block in range(blocks):
                for member in range(members):
                    tall[block, member * share : (member + 1) * share, :] = chunk[
                        member, block * share : (block + 1) * share, :
                    ]
                wholes[pl.ds(base, height), block * LANES : (block + 1) * LANES] = tall[
                    block
                ].astype(jnp.bfloat16)

        store(part).start()
    for part in range(parts):
        store(part).wait()


def chunk_rows(arrived, hidden, width, parts=4, members=8):
    slots, height, _ = arrived.shape
    blocks = width // LANES
    share = height // blocks
    return pl.pallas_call(
        rows_kernel,
        out_shape=jax.ShapeDtypeStruct((hidden, width), jnp.bfloat16),
        in_specs=[NEAR],
        out_specs=FAR,
        scratch_shapes=[
            pltpu.VMEM((hidden, width), jnp.bfloat16),
            pltpu.VMEM((members, height, LANES), jnp.float32),
            pltpu.VMEM((blocks, members * share, LANES), jnp.float32),
            pltpu.SemaphoreType.DMA((parts,)),
        ],
        compiler_params=pltpu.CompilerParams(vmem_limit_bytes=32 << 20),
        name="chunk_rows",
    )(pltpu.with_memory_space_constraint(arrived, pltpu.VMEM))


def exchange(chunks):
    return lax.all_to_all(chunks, "dev", split_axis=0, concat_axis=0, tiled=True)


def per_device(saved, cotangent, weights, counts, live_rows, next_map, master, moment1, moment2):
    cot_rows = cotangent[0]
    devices = lax.axis_size("dev")
    experts, share, width = master.shape
    hidden = saved.shape[2]
    row_count = saved.shape[1]
    chunks = slot_chunks(saved[0], cot_rows, live_rows, devices)
    received = exchange(chunks)
    row_index = jnp.arange(row_count, dtype=jnp.int32)
    masked = jnp.where(
        (row_index < live_rows[0])[:, None], cot_rows, jnp.zeros_like(cot_rows)
    )
    input_grads = contract_cols(masked, weights[0]).astype(jnp.bfloat16)
    slot_index = jnp.arange(devices, dtype=jnp.int32)
    bounds = jnp.cumsum(counts)
    holders = jnp.sum((bounds[None, :] <= slot_index[:, None]).astype(jnp.int32), axis=1)
    fresh = jnp.any(bounds[None, :] == slot_index[:, None], axis=1) | (slot_index == 0)
    new_master, new_one, new_two, outgoing = adam_step(
        holders, fresh.astype(jnp.int32), next_map, received,
        master.transpose(1, 0, 2), moment1.transpose(1, 0, 2), moment2.transpose(1, 0, 2),
    )
    arriving = exchange(outgoing)
    next_weights = chunk_rows(arriving, hidden, width)
    return (
        input_grads[None],
        new_master.transpose(1, 0, 2),
        new_one.transpose(1, 0, 2),
        new_two.transpose(1, 0, 2),
        next_weights[None],
    )


def solution(mesh):
    placed = (
        P("dev", None, None),
        P("dev", None, None),
        P("dev", None, None),
        P(),
        P("dev"),
        P(),
        P(None, "dev", None),
        P(None, "dev", None),
        P(None, "dev", None),
    )
    return jax.shard_map(
        per_device,
        mesh=mesh,
        in_specs=placed,
        out_specs=(
            P("dev", None, None),
            P(None, "dev", None),
            P(None, "dev", None),
            P(None, "dev", None),
            P("dev", None, None),
        ),
        check_vma=False,
    )
```

profile of v0, /device:TPU:1, one launch (start us, length us, event | category | flops | bytes accessed | tf_op | source)
XLA Modules:
  0.0 120.0 jit_solution(10010626704941421579)
XLA Ops:
  1.3 8.5 %slot_chunks.1 = bf16[128,96,128]{2,1,0:T(8,128)(2,1)} custom-call(s32[1]{0:T(128)} %copy.17.live_ref, bf16[1024,768]{1,0:T(8,128)(2,1)} %bitcast.35, bf16[1024,2048]{1,0:T(8,128)(2,1)} %bitcast.33), custom_call_target="tpu_custom_call" | custom-call | flops 3221225472 | bytes 8912896 | tf_op jit(solution)/shard_map/slot_chunks/pallas_call | solution.py:119
  9.8 0.0 copy-start
  9.8 11.5 %all-to-all-start = ((bf16[128,96,128]{2,1,0:T(8,128)(2,1)}), bf16[128,96,128]{2,1,0:T(8,128)(2,1)S(1)}, u32[]{:S(2)}, u32[]{:S(2)}) async-start(bf16[128,96,128]{2,1,0:T(8,128)(2,1)} %slot_chunks.1), calls=%async_computation | async-start | bytes 6291456 | tf_op jit(solution)/shard_map/all_to_all | solution.py:337
  21.3 0.0 copy-done
  21.3 0.1 copy.16
  21.4 0.1 reduce-window.8
  21.5 0.1 reduce
  21.6 0.1 fusion.16
  21.7 0.7 convert_reduce_fusion.holder_ref
  22.4 0.5 or_convert_fusion.fresh_ref
  22.9 40.0 %all-to-all-done.pieces = bf16[128,96,128]{2,1,0:T(8,128)(2,1)S(1)} async-done(((bf16[128,96,128]{2,1,0:T(8,128)(2,1)}), bf16[128,96,128]{2,1,0:T(8,128)(2,1)S(1)}, u32[]{:S(2)}, u32[]{:S(2)}) %all-to-all-start) | async-done | bytes 3145760 | tf_op jit(solution)/shard_map/all_to_all | solution.py:337
  62.9 7.9 %adam_step.1 = (f32[6,64,2048]{2,1,0:T(8,128)}, bf16[6,64,2048]{2,1,0:T(8,128)(2,1)}, bf16[6,64,2048]{2,1,0:T(8,128)(2,1)}, bf16[128,96,128]{2,1,0:T(8,128)(2,1)}) custom-call(s32[128]{0:T(128)} %convert_reduce_fusion.holder_ref, s32[128]{0:T(128)} %or_convert_fusion.fresh_ref, s32[128]{0:T(128)} %next_ref.1, bf16[128,96,128]{2,1,0:T(8,128)(2,1)S(1)} %all-to-all-done.pieces, ...), custom_call_target="tpu_custom_call" | custom-call | tf_op jit(solution)/shard_map/adam_step/pallas_call | solution.py:253
  70.8 4.6 %all-to-all-start.1 = ((bf16[128,96,128]{2,1,0:T(8,128)(2,1)}), bf16[128,96,128]{2,1,0:T(8,128)(2,1)S(1)}, u32[]{:S(2)}, u32[]{:S(2)}) async-start(bf16[128,96,128]{2,1,0:T(8,128)(2,1)} %get-tuple-element.12), calls=%async_computation.1 | async-start | bytes 6291456 | tf_op jit(solution)/shard_map/all_to_all | solution.py:337
  75.4 7.8 %fusion.11 = bf16[1,1024,768]{2,1,0:T(8,128)(2,1)} fusion(bf16[1,768,2048]{2,1,0:T(8,128)(2,1)} %param.11, bf16[1,1024,2048]{2,1,0:T(8,128)(2,1)} %param.10, pred[1024]{0:T(1024)(128)(4,1)S(1)} %iota_compare_fusion.2), kind=kOutput, calls=%fused_computation.7 | convolution fusion | flops 3224109056 | bytes 8913920 | tf_op jit(solution)/shard_map/dot_general | solution.py:22
  83.2 33.9 %all-to-all-done.1.arrived = bf16[128,96,128]{2,1,0:T(8,128)(2,1)S(1)} async-done(((bf16[128,96,128]{2,1,0:T(8,128)(2,1)}), bf16[128,96,128]{2,1,0:T(8,128)(2,1)S(1)}, u32[]{:S(2)}, u32[]{:S(2)}) %all-to-all-start.1) | async-done | bytes 3145760 | tf_op jit(solution)/shard_map/all_to_all | solution.py:337
  117.2 2.9 %chunk_rows.1 = bf16[768,2048]{1,0:T(8,128)(2,1)} custom-call(bf16[128,96,128]{2,1,0:T(8,128)(2,1)S(1)} %all-to-all-done.1.arrived), custom_call_target="tpu_custom_call" | custom-call | tf_op jit(solution)/shard_map/chunk_rows/pallas_call | solution.py:320
  (1 shorter events, 0.0 us)
Async XLA Ops:
  9.8 11.5 %copy-start = (s32[64]{0:T(128)S(1)}, s32[64]{0:T(128)}, u32[]{:S(2)}) copy-start(s32[64]{0:T(128)} %param.12) | copy-start | bytes 772
  9.8 53.1 %all-to-all-start = ((bf16[128,96,128]{2,1,0:T(8,128)(2,1)}), bf16[128,96,128]{2,1,0:T(8,128)(2,1)S(1)}, u32[]{:S(2)}, u32[]{:S(2)}) async-start(bf16[128,96,128]{2,1,0:T(8,128)(2,1)} %slot_chunks.1), calls=%async_computation | async-start | bytes 6291456 | tf_op jit(solution)/shard_map/all_to_all | solution.py:337
  70.8 46.4 %all-to-all-start.1 = ((bf16[128,96,128]{2,1,0:T(8,128)(2,1)}), bf16[128,96,128]{2,1,0:T(8,128)(2,1)S(1)}, u32[]{:S(2)}, u32[]{:S(2)}) async-start(bf16[128,96,128]{2,1,0:T(8,128)(2,1)} %get-tuple-element.12), calls=%async_computation.1 | async-start | bytes 6291456 | tf_op jit(solution)/shard_map/all_to_all | solution.py:337
where the time goes:
time: 120 us
  waiting for transfers between devices  73.9 us (62%)
  Pallas kernels  19.2 us (16%)
  starting transfers between devices  16.1 us (13%)
  matrix products  7.78 us (6%)
  other arithmetic  1.5 us (1%)
  between operations  1.34 us (1%)
    all_to_all x2, waiting for transfers between devices, exchange(): lax.all_to_all(chunks, 'dev', split_axis=0, concat_axis=0, tiled=True)  73.9 us
    all_to_all x2, starting transfers between devices, exchange(): lax.all_to_all(chunks, 'dev', split_axis=0, concat_axis=0, tiled=True)  16.1 us
    pallas_call x1, Pallas kernels, slot_chunks(): pl.pallas_call(grads_kernel, out_shape=jax.ShapeDtypeStruct((devices, blo...  8.51 us
    pallas_call x1, Pallas kernels, adam_step(): pl.pallas_call(adam_kernel, out_shape=(pltpu.HBM(master.shape, jnp.float3...  7.87 us
    dot_general x1, matrix products, contract_cols(): lax.dot_general(left, right, (((1,), (1,)), ((), ())), preferred_element_...  7.78 us
    pallas_call x1, Pallas kernels, chunk_rows(): pl.pallas_call(rows_kernel, out_shape=jax.ShapeDtypeStruct((hidden, width...  2.86 us
  transfers between devices with their start and end apart: 2, of which 2 were waited for; matrix products, arithmetic and copies ran while one was open for 8% of the time, Pallas kernels for 0%

commit v1 on v0

--- a/solution.py
+++ b/solution.py
@@ -31,15 +31,12 @@
 
 def grads_kernel(
     live_ref, saved_ref, cot_ref, out_ref,
-    saved_in, cot_in, turned, sums, chunk, packed, saved_sem, cot_sem, out_sem,
+    live, saved_in, cot_in, turned, spread, packed, live_sem, saved_sem, cot_sem, out_sem,
 ):
     rows, hidden = saved_ref.shape
     steps, _, wide = cot_in.shape
-    blocks = sums.shape[0]
-    per_step = wide // LANES
     devices = out_ref.shape[0]
     share = hidden // devices
-    tall = GROUP * share
     parts = out_sem.shape[0]
     part_size = devices // parts
     bands = saved_sem.shape[0]
@@ -58,8 +55,11 @@
         span = pl.ds(part * part_size, part_size)
         return pltpu.make_async_copy(packed.at[span], out_ref.at[span], out_sem.at[part])
 
+    load_live = pltpu.make_async_copy(live_ref, live, live_sem.at[0])
+    load_live.start()
     for band in range(bands):
         load_saved(band).start()
+    load_live.wait()
 
     @pl.loop(0, bands)
     def _(band):
@@ -68,18 +68,28 @@
 
         @pl.when(band == 0)
         def _():
-            for step in range(steps):
-                load_cot(step).start()
+            load_cot(0).start()
 
         index = lax.broadcasted_iota(jnp.int32, (band_rows, hidden), 0)
         part = saved_in[span, :]
         turned[:, span] = jnp.where(
-            index < live_ref[0] - band * band_rows, part, jnp.zeros_like(part)
+            index < live[0] - band * band_rows, part, jnp.zeros_like(part)
         ).T
+
+    load_cot(1).start()
 
     @pl.loop(0, steps)
     def _(step):
         pltpu.make_async_copy(cot_ref.at[:, :wide], cot_in.at[step], cot_sem.at[step]).wait()
+
+        @pl.when(step + 2 < steps)
+        def _():
+            later = step + 2
+            span = pl.ds(pl.multiple_of(later * wide, wide), wide)
+            pltpu.make_async_copy(
+                cot_ref.at[:, span], cot_in.at[later], cot_sem.at[later]
+            ).start()
+
         for start in range(0, wide, 2 * LANES):
             product = jnp.dot(
                 turned[...],
@@ -87,23 +97,21 @@
                 preferred_element_type=jnp.float32,
             )
             for part in range(2):
-                sums[step * per_step + start // LANES + part] = product[
-                    :, part * LANES : (part + 1) * LANES
-                ]
+                block = start // LANES + part
+                for device in range(devices):
+                    spread[step, device, block * share : (block + 1) * share, :] = product[
+                        device * share : (device + 1) * share, part * LANES : (part + 1) * LANES
+                    ]
 
     for part in range(parts):
 
         @pl.loop(part * part_size // GROUP, (part + 1) * part_size // GROUP)
         def _(group):
-            base = pl.multiple_of(group * tall, 8)
-            for block in range(blocks):
-                piece = sums[block, pl.ds(base, tall), :]
-                for member in range(GROUP):
-                    chunk[member, block * share : (block + 1) * share, :] = piece[
-                        member * share : (member + 1) * share, :
-                    ]
             for member in range(GROUP):
-                packed[group * GROUP + member] = chunk[member].astype(jnp.bfloat16)
+                device = group * GROUP + member
+                packed[device] = jnp.concatenate(
+                    [spread[step, device] for step in range(steps)], axis=0
+                ).astype(jnp.bfloat16)
 
         send(part).start()
     for part in range(parts):
@@ -119,15 +127,16 @@
     return pl.pallas_call(
         grads_kernel,
         out_shape=jax.ShapeDtypeStruct((devices, blocks * share, LANES), jnp.bfloat16),
-        in_specs=[SCALARS, FAR, FAR],
+        in_specs=[FAR, FAR, FAR],
         out_specs=FAR,
         scratch_shapes=[
+            pltpu.SMEM((1,), jnp.int32),
             pltpu.VMEM((rows, hidden), jnp.bfloat16),
             pltpu.VMEM((steps, rows, wide), jnp.bfloat16),
             pltpu.VMEM((hidden, rows), jnp.bfloat16),
-            pltpu.VMEM((blocks, hidden, LANES), jnp.float32),
-            pltpu.VMEM((GROUP, blocks * share, LANES), jnp.float32),
+            pltpu.VMEM((steps, devices, wide // LANES * share, LANES), jnp.float32),
             pltpu.VMEM((devices, blocks * share, LANES), jnp.bfloat16),
+            pltpu.SemaphoreType.DMA((1,)),
             pltpu.SemaphoreType.DMA((bands,)),
             pltpu.SemaphoreType.DMA((steps,)),
             pltpu.SemaphoreType.DMA((parts,)),
@@ -153,6 +162,7 @@
     deep = 16
     tiles = experts // deep
     quad = GROUP * share
+    pitch = sums.shape[0] // experts
     arrays = ((master_ref, master, master_out), (one_ref, one, one_out), (two_ref, two, two_out))
     sends = send_sem.shape[0]
     send_size = slots // sends
@@ -181,7 +191,7 @@
 
     def add_slot(slot, total):
         total = jnp.where(fresh_ref[slot] > 0, 0.0, total) + pieces[slot].astype(jnp.float32)
-        sums[holder_ref[slot]] = total
+        sums[pl.ds(holder_ref[slot] * pitch, height), :] = total
         return total
 
     lax.fori_loop(0, slots, add_slot, jnp.zeros((height, LANES), jnp.float32), unroll=4)
@@ -194,38 +204,27 @@
 
         @pl.loop(0, blocks // GROUP)
         def _(four):
-            def place(half, band):
-                return (
-                    pl.ds(tile * deep + half * 8, 8),
-                    pl.ds(pl.multiple_of(four * quad + band * 8, 8), 8),
+            for k in range(quad):
+                block, row = divmod(k, share)
+                place = pl.ds(tile * (deep * pitch) + four * quad + k, deep, stride=pitch)
+                lanes = pl.ds(pl.multiple_of((four * GROUP + block) * LANES, LANES), LANES)
+                grad = sums[place, :]
+                first = (
+                    BETA_ONE * one[row, rows, lanes].astype(jnp.float32)
+                    + (1.0 - BETA_ONE) * grad
                 )
-
-            for band in range(quad // 8):
-                turned = [jnp.swapaxes(sums[place(half, band)], 0, 1) for half in range(2)]
-                fresh = ([], [])
-                for k in range(8):
-                    block, row = divmod(band * 8 + k, share)
-                    grad = jnp.concatenate([turned[0][k], turned[1][k]], axis=0)
-                    lanes = pl.ds(pl.multiple_of((four * GROUP + block) * LANES, LANES), LANES)
-                    first = (
-                        BETA_ONE * one[row, rows, lanes].astype(jnp.float32)
-                        + (1.0 - BETA_ONE) * grad
-                    )
-                    second = (
-                        BETA_TWO * two[row, rows, lanes].astype(jnp.float32)
-                        + (1.0 - BETA_TWO) * (grad * grad)
-                    )
-                    root = second * lax.rsqrt(second) * BIAS_TWO**-0.5 + EPSILON
-                    new = (1.0 - LEARN_RATE * DECAY_RATE) * master[row, rows, lanes] - (
-                        (LEARN_RATE / BIAS_ONE) * first
-                    ) / root
-                    master[row, rows, lanes] = new
-                    one[row, rows, lanes] = first.astype(jnp.bfloat16)
-                    two[row, rows, lanes] = second.astype(jnp.bfloat16)
-                    fresh[0].append(new[:8])
-                    fresh[1].append(new[8:])
-                for half in range(2):
-                    sums[place(half, band)] = jnp.swapaxes(jnp.stack(fresh[half]), 0, 1)
+                second = (
+                    BETA_TWO * two[row, rows, lanes].astype(jnp.float32)
+                    + (1.0 - BETA_TWO) * (grad * grad)
+                )
+                root = second * lax.rsqrt(second) + EPSILON * BIAS_TWO**0.5
+                new = (1.0 - LEARN_RATE * DECAY_RATE) * master[row, rows, lanes] - (
+                    (LEARN_RATE / BIAS_ONE * BIAS_TWO**0.5) * first
+                ) / root
+                master[row, rows, lanes] = new
+                one[row, rows, lanes] = first.astype(jnp.bfloat16)
+                two[row, rows, lanes] = second.astype(jnp.bfloat16)
+                sums[place, :] = new
 
         for copy in stores(tile):
             copy.start()
@@ -233,7 +232,7 @@
     for part in range(sends):
 
         def fill(slot, carry):
-            outgoing[slot] = sums[next_ref[slot]].astype(jnp.bfloat16)
+            outgoing[slot] = sums[pl.ds(next_ref[slot] * pitch, height), :].astype(jnp.bfloat16)
             return carry
 
         lax.fori_loop(part * send_size, (part + 1) * send_size, fill, 0, unroll=4)
@@ -261,7 +260,7 @@
         in_specs=[SCALARS] * 3 + [NEAR] + [FAR] * 3,
         out_specs=(FAR,) * 4,
         scratch_shapes=[
-            pltpu.VMEM((experts, height, LANES), jnp.float32),
+            pltpu.VMEM((experts * (height + 1), LANES), jnp.float32),
             pltpu.VMEM(master.shape, jnp.float32),
             pltpu.VMEM(one.shape, jnp.bfloat16),
             pltpu.VMEM(two.shape, jnp.bfloat16),
@@ -278,13 +277,13 @@
     )
 
 
-def rows_kernel(arrived, out_ref, wholes, chunk, tall, out_sem):
+def rows_kernel(arrived, out_ref, wholes, tall, out_sem):
     slots, depth, _ = arrived.shape
     width = out_ref.shape[1]
-    members = chunk.shape[0]
     blocks = width // LANES
     share = depth // blocks
-    height = members * share
+    height = tall.shape[1]
+    members = height // share
     parts = out_sem.shape[0]
     part_size = slots // parts
 
@@ -296,14 +295,14 @@
 
         @pl.loop(part * part_size // members, (part + 1) * part_size // members)
         def _(group):
+            base = pl.multiple_of(group * height, 16)
             for member in range(members):
-                chunk[member] = arrived[group * members + member].astype(jnp.float32)
-            base = pl.multiple_of(group * height, 16)
+                chunk = arrived[group * members + member].astype(jnp.float32)
+                for block in range(blocks):
+                    tall[block, member * share : (member + 1) * share, :] = chunk[
+                        block * share : (block + 1) * share, :
+                    ]
             for block in range(blocks):
-                for member in range(members):
-                    tall[block, member * share : (member + 1) * share, :] = chunk[
-                        member, block * share : (block + 1) * share, :
-                    ]
                 wholes[pl.ds(base, height), block * LANES : (block + 1) * LANES] = tall[
                     block
                 ].astype(jnp.bfloat16)
@@ -324,7 +323,6 @@
         out_specs=FAR,
         scratch_shapes=[
             pltpu.VMEM((hidden, width), jnp.bfloat16),
-            pltpu.VMEM((members, height, LANES), jnp.float32),
             pltpu.VMEM((blocks, members * share, LANES), jnp.float32),
             pltpu.SemaphoreType.DMA((parts,)),
         ],

time: 120 us -> 118 us (0.983)
  Pallas kernels: 19.2 us -> 17.1 us
where the time goes in v1:
time: 118 us
  waiting for transfers between devices  73.9 us (63%)
  Pallas kernels  17.1 us (14%)
  starting transfers between devices  16.1 us (14%)
  matrix products  7.78 us (7%)
  other arithmetic  1.5 us (1%)
  between operations  1.34 us (1%)
    all_to_all x2, waiting for transfers between devices, exchange(): lax.all_to_all(chunks, 'dev', split_axis=0, concat_axis=0, tiled=True)  73.9 us
    all_to_all x2, starting transfers between devices, exchange(): lax.all_to_all(chunks, 'dev', split_axis=0, concat_axis=0, tiled=True)  16.1 us
    pallas_call x1, Pallas kernels, slot_chunks(): pl.pallas_call(grads_kernel, out_shape=jax.ShapeDtypeStruct((devices, blo...  8.13 us
    dot_general x1, matrix products, contract_cols(): lax.dot_general(left, right, (((1,), (1,)), ((), ())), preferred_element_...  7.78 us
    pallas_call x1, Pallas kernels, adam_step(): pl.pallas_call(adam_kernel, out_shape=(pltpu.HBM(master.shape, jnp.float3...  6.78 us
  transfers between devices with their start and end apart: 2, of which 2 were waited for; matrix products, arithmetic and copies ran while one was open for 8% of the time, Pallas kernels for 0%

profile of v1, /device:TPU:1, one launch (start us, length us, event | category | flops | bytes accessed | tf_op | source)
XLA Modules:
  0.0 117.9 jit_solution(10296502834612605664)
XLA Ops:
  1.3 8.1 %slot_chunks.1 = bf16[128,96,128]{2,1,0:T(8,128)(2,1)} custom-call(s32[1]{0:T(128)} %copy.17.live_ref, bf16[1024,768]{1,0:T(8,128)(2,1)} %bitcast.35, bf16[1024,2048]{1,0:T(8,128)(2,1)} %bitcast.33), custom_call_target="tpu_custom_call" | custom-call | flops 3221225472 | bytes 8912896 | tf_op jit(solution)/shard_map/slot_chunks/pallas_call | solution.py:127
  9.4 0.0 copy-start
  9.4 11.5 %all-to-all-start = ((bf16[128,96,128]{2,1,0:T(8,128)(2,1)}), bf16[128,96,128]{2,1,0:T(8,128)(2,1)S(1)}, u32[]{:S(2)}, u32[]{:S(2)}) async-start(bf16[128,96,128]{2,1,0:T(8,128)(2,1)} %slot_chunks.1), calls=%async_computation | async-start | bytes 6291456 | tf_op jit(solution)/shard_map/all_to_all | solution.py:335
  20.9 0.0 copy-done
  20.9 0.1 copy.16
  21.0 0.1 reduce-window.8
  21.1 0.1 reduce
  21.2 0.1 fusion.16
  21.3 0.7 convert_reduce_fusion.holder_ref
  22.0 0.5 or_convert_fusion.fresh_ref
  22.5 40.0 %all-to-all-done.pieces = bf16[128,96,128]{2,1,0:T(8,128)(2,1)S(1)} async-done(((bf16[128,96,128]{2,1,0:T(8,128)(2,1)}), bf16[128,96,128]{2,1,0:T(8,128)(2,1)S(1)}, u32[]{:S(2)}, u32[]{:S(2)}) %all-to-all-start) | async-done | bytes 3145760 | tf_op jit(solution)/shard_map/all_to_all | solution.py:335
  62.5 6.8 %adam_step.1 = (f32[6,64,2048]{2,1,0:T(8,128)}, bf16[6,64,2048]{2,1,0:T(8,128)(2,1)}, bf16[6,64,2048]{2,1,0:T(8,128)(2,1)}, bf16[128,96,128]{2,1,0:T(8,128)(2,1)}) custom-call(s32[128]{0:T(128)} %convert_reduce_fusion.holder_ref, s32[128]{0:T(128)} %or_convert_fusion.fresh_ref, s32[128]{0:T(128)} %next_ref.1, bf16[128,96,128]{2,1,0:T(8,128)(2,1)S(1)} %all-to-all-done.pieces, ...), custom_call_target="tpu_custom_call" | custom-call | tf_op jit(solution)/shard_map/adam_step/pallas_call | solution.py:252
  69.3 4.6 %all-to-all-start.1 = ((bf16[128,96,128]{2,1,0:T(8,128)(2,1)}), bf16[128,96,128]{2,1,0:T(8,128)(2,1)S(1)}, u32[]{:S(2)}, u32[]{:S(2)}) async-start(bf16[128,96,128]{2,1,0:T(8,128)(2,1)} %get-tuple-element.12), calls=%async_computation.1 | async-start | bytes 6291456 | tf_op jit(solution)/shard_map/all_to_all | solution.py:335
  74.0 7.8 %fusion.11 = bf16[1,1024,768]{2,1,0:T(8,128)(2,1)} fusion(bf16[1,768,2048]{2,1,0:T(8,128)(2,1)} %param.11, bf16[1,1024,2048]{2,1,0:T(8,128)(2,1)} %param.10, pred[1024]{0:T(1024)(128)(4,1)S(1)} %iota_compare_fusion.2), kind=kOutput, calls=%fused_computation.7 | convolution fusion | flops 3224109056 | bytes 8913920 | tf_op jit(solution)/shard_map/dot_general | solution.py:22
  81.7 33.9 %all-to-all-done.1.arrived = bf16[128,96,128]{2,1,0:T(8,128)(2,1)S(1)} async-done(((bf16[128,96,128]{2,1,0:T(8,128)(2,1)}), bf16[128,96,128]{2,1,0:T(8,128)(2,1)S(1)}, u32[]{:S(2)}, u32[]{:S(2)}) %all-to-all-start.1) | async-done | bytes 3145760 | tf_op jit(solution)/shard_map/all_to_all | solution.py:335
  115.7 2.2 %chunk_rows.1 = bf16[768,2048]{1,0:T(8,128)(2,1)} custom-call(bf16[128,96,128]{2,1,0:T(8,128)(2,1)S(1)} %all-to-all-done.1.arrived), custom_call_target="tpu_custom_call" | custom-call | tf_op jit(solution)/shard_map/chunk_rows/pallas_call | solution.py:319
  (1 shorter events, 0.0 us)
Async XLA Ops:
  9.4 11.5 %copy-start = (s32[64]{0:T(128)S(1)}, s32[64]{0:T(128)}, u32[]{:S(2)}) copy-start(s32[64]{0:T(128)} %param.12) | copy-start | bytes 772
  9.4 53.1 %all-to-all-start = ((bf16[128,96,128]{2,1,0:T(8,128)(2,1)}), bf16[128,96,128]{2,1,0:T(8,128)(2,1)S(1)}, u32[]{:S(2)}, u32[]{:S(2)}) async-start(bf16[128,96,128]{2,1,0:T(8,128)(2,1)} %slot_chunks.1), calls=%async_computation | async-start | bytes 6291456 | tf_op jit(solution)/shard_map/all_to_all | solution.py:335
  69.3 46.4 %all-to-all-start.1 = ((bf16[128,96,128]{2,1,0:T(8,128)(2,1)}), bf16[128,96,128]{2,1,0:T(8,128)(2,1)S(1)}, u32[]{:S(2)}, u32[]{:S(2)}) async-start(bf16[128,96,128]{2,1,0:T(8,128)(2,1)} %get-tuple-element.12), calls=%async_computation.1 | async-start | bytes 6291456 | tf_op jit(solution)/shard_map/all_to_all | solution.py:335

commit v2 on v1

--- a/solution.py
+++ b/solution.py
@@ -31,14 +31,15 @@
 
 def grads_kernel(
     live_ref, saved_ref, cot_ref, out_ref,
-    live, saved_in, cot_in, turned, spread, packed, live_sem, saved_sem, cot_sem, out_sem,
+    saved_in, cot_in, turned, ordered, packed, saved_sem, cot_sem, out_sem,
 ):
     rows, hidden = saved_ref.shape
-    steps, _, wide = cot_in.shape
+    strips, _, thin = cot_in.shape
+    steps = packed.shape[0]
+    per_step = strips // steps
     devices = out_ref.shape[0]
     share = hidden // devices
-    parts = out_sem.shape[0]
-    part_size = devices // parts
+    tall = ordered.shape[1]
     bands = saved_sem.shape[0]
     band_rows = rows // bands
 
@@ -46,20 +47,33 @@
         span = pl.ds(band * band_rows, band_rows)
         return pltpu.make_async_copy(saved_ref.at[span], saved_in.at[span], saved_sem.at[band])
 
-    def load_cot(step):
-        return pltpu.make_async_copy(
-            cot_ref.at[:, step * wide : (step + 1) * wide], cot_in.at[step], cot_sem.at[step]
-        )
-
-    def send(part):
-        span = pl.ds(part * part_size, part_size)
-        return pltpu.make_async_copy(packed.at[span], out_ref.at[span], out_sem.at[part])
-
-    load_live = pltpu.make_async_copy(live_ref, live, live_sem.at[0])
-    load_live.start()
+    def load_cot(strip):
+        span = pl.ds(strip * thin, thin)
+        return pltpu.make_async_copy(cot_ref.at[:, span], cot_in.at[strip], cot_sem.at[strip])
+
+    def send(step):
+        span = pl.ds(pl.multiple_of(step * tall, tall), tall)
+        return pltpu.make_async_copy(packed.at[step], out_ref.at[:, span], out_sem.at[step])
+
+    def multiply(step, target):
+        for which in range(per_step):
+            strip = step * per_step + which
+            pltpu.make_async_copy(
+                cot_ref.at[:, :thin], cot_in.at[strip], cot_sem.at[strip]
+            ).wait()
+        for which in range(per_step):
+            product = jnp.dot(
+                turned[...], cot_in[step * per_step + which], preferred_element_type=jnp.float32
+            )
+            for part in range(thin // LANES):
+                block = which * (thin // LANES) + part
+                for device in range(devices):
+                    target[device, block * share : (block + 1) * share, :] = product[
+                        device * share : (device + 1) * share, part * LANES : (part + 1) * LANES
+                    ]
+
     for band in range(bands):
         load_saved(band).start()
-    load_live.wait()
 
     @pl.loop(0, bands)
     def _(band):
@@ -68,78 +82,55 @@
 
         @pl.when(band == 0)
         def _():
-            load_cot(0).start()
+            for strip in range(per_step):
+                load_cot(strip).start()
 
         index = lax.broadcasted_iota(jnp.int32, (band_rows, hidden), 0)
         part = saved_in[span, :]
         turned[:, span] = jnp.where(
-            index < live[0] - band * band_rows, part, jnp.zeros_like(part)
+            index < live_ref[0] - band * band_rows, part, jnp.zeros_like(part)
         ).T
 
-    load_cot(1).start()
+    for strip in range(per_step, strips):
+        load_cot(strip).start()
 
     @pl.loop(0, steps)
     def _(step):
-        pltpu.make_async_copy(cot_ref.at[:, :wide], cot_in.at[step], cot_sem.at[step]).wait()
-
-        @pl.when(step + 2 < steps)
-        def _():
-            later = step + 2
-            span = pl.ds(pl.multiple_of(later * wide, wide), wide)
-            pltpu.make_async_copy(
-                cot_ref.at[:, span], cot_in.at[later], cot_sem.at[later]
-            ).start()
-
-        for start in range(0, wide, 2 * LANES):
-            product = jnp.dot(
-                turned[...],
-                cot_in[step, :, start : start + 2 * LANES],
-                preferred_element_type=jnp.float32,
-            )
-            for part in range(2):
-                block = start // LANES + part
-                for device in range(devices):
-                    spread[step, device, block * share : (block + 1) * share, :] = product[
-                        device * share : (device + 1) * share, part * LANES : (part + 1) * LANES
-                    ]
-
-    for part in range(parts):
-
-        @pl.loop(part * part_size // GROUP, (part + 1) * part_size // GROUP)
-        def _(group):
-            for member in range(GROUP):
-                device = group * GROUP + member
-                packed[device] = jnp.concatenate(
-                    [spread[step, device] for step in range(steps)], axis=0
-                ).astype(jnp.bfloat16)
-
-        send(part).start()
-    for part in range(parts):
-        send(part).wait()
-
-
-def slot_chunks(saved, cot, live, devices, steps=4, parts=4, bands=4):
+        multiply(step, ordered)
+
+        @pl.loop(0, devices // 8)
+        def _(eight):
+            for member in range(8):
+                packed[step, eight * 8 + member] = ordered[eight * 8 + member].astype(jnp.bfloat16)
+
+        send(step).start()
+
+    for step in range(steps):
+        send(step).wait()
+
+
+def slot_chunks(saved, cot, live, devices, steps=4, bands=4):
     rows, hidden = saved.shape
     width = cot.shape[1]
-    wide = width // steps
+    thin = 2 * LANES
+    strips = width // thin
     share = hidden // devices
     blocks = width // LANES
+    tall = blocks // steps * share
     return pl.pallas_call(
         grads_kernel,
         out_shape=jax.ShapeDtypeStruct((devices, blocks * share, LANES), jnp.bfloat16),
-        in_specs=[FAR, FAR, FAR],
+        in_specs=[SCALARS, FAR, FAR],
         out_specs=FAR,
         scratch_shapes=[
-            pltpu.SMEM((1,), jnp.int32),
             pltpu.VMEM((rows, hidden), jnp.bfloat16),
-            pltpu.VMEM((steps, rows, wide), jnp.bfloat16),
+            pltpu.VMEM((strips, rows, thin), jnp.bfloat16),
             pltpu.VMEM((hidden, rows), jnp.bfloat16),
-            pltpu.VMEM((steps, devices, wide // LANES * share, LANES), jnp.float32),
-            pltpu.VMEM((devices, blocks * share, LANES), jnp.bfloat16),
-            pltpu.SemaphoreType.DMA((1,)),
+            pltpu.VMEM((devices, tall, LANES), jnp.float32),
+            pltpu.VMEM((steps, devices, tall, LANES), jnp.bfloat16),
             pltpu.SemaphoreType.DMA((bands,)),
+            pltpu.SemaphoreType.DMA((strips,)),
             pltpu.SemaphoreType.DMA((steps,)),
-            pltpu.SemaphoreType.DMA((parts,)),
         ],
         compiler_params=pltpu.CompilerParams(vmem_limit_bytes=63 << 20),
         cost_estimate=pl.CostEstimate(
@@ -151,10 +142,43 @@
     )(live, saved, cot)
 
 
+def inputs_kernel(live_ref, cot_ref, weights_ref, out_ref):
+    tall = cot_ref.shape[0]
+    index = lax.broadcasted_iota(jnp.int32, out_ref.shape, 0) + pl.program_id(0) * tall
+    product = contract_cols(cot_ref[...], weights_ref[...])
+    out_ref[...] = jnp.where(index < live_ref[0], product, 0.0).astype(jnp.bfloat16)
+
+
+def input_rows(cot, weights, live, steps=4):
+    rows, width = cot.shape
+    hidden = weights.shape[0]
+    return pl.pallas_call(
+        inputs_kernel,
+        out_shape=jax.ShapeDtypeStruct((rows, hidden), jnp.bfloat16),
+        grid=(steps,),
+        in_specs=[
+            SCALARS,
+            pl.BlockSpec((rows // steps, width), lambda i: (i, 0)),
+            pl.BlockSpec((hidden, width), lambda i: (0, 0)),
+        ],
+        out_specs=pl.BlockSpec((rows // steps, hidden), lambda i: (i, 0)),
+        compiler_params=pltpu.CompilerParams(
+            dimension_semantics=("arbitrary",), vmem_limit_bytes=40 << 20
+        ),
+        cost_estimate=pl.CostEstimate(
+            flops=2 * rows * hidden * width,
+            bytes_accessed=2 * (rows * hidden + rows * width + hidden * width),
+            transcendentals=0,
+        ),
+        name="input_rows",
+    )(live, cot, weights)
+
+
 def adam_kernel(
-    holder_ref, fresh_ref, next_ref, pieces, master_ref, one_ref, two_ref,
+    holder_far, fresh_far, next_far, pieces, master_ref, one_ref, two_ref,
     master_out, one_out, two_out, send_out,
-    sums, master, one, two, outgoing, load_sem, store_sem, send_sem,
+    holder_ref, fresh_ref, next_ref, sums, master, one, two, outgoing,
+    table_sem, load_sem, store_sem, send_sem,
 ):
     slots, height, _ = pieces.shape
     share, experts, width = master_ref.shape
@@ -185,9 +209,19 @@
         span = pl.ds(part * send_size, send_size)
         return pltpu.make_async_copy(outgoing.at[span], send_out.at[span], send_sem.at[part])
 
+    tables = [
+        pltpu.make_async_copy(far, near, table_sem.at[which])
+        for which, (far, near) in enumerate(
+            ((holder_far, holder_ref), (fresh_far, fresh_ref), (next_far, next_ref))
+        )
+    ]
+    for copy in tables:
+        copy.start()
     for tile in range(tiles):
         for copy in loads(tile):
             copy.start()
+    for copy in tables:
+        copy.wait()
 
     def add_slot(slot, total):
         total = jnp.where(fresh_ref[slot] > 0, 0.0, total) + pieces[slot].astype(jnp.float32)
@@ -257,14 +291,18 @@
             pltpu.HBM(two.shape, jnp.bfloat16),
             pltpu.HBM((slots, height, LANES), jnp.bfloat16),
         ),
-        in_specs=[SCALARS] * 3 + [NEAR] + [FAR] * 3,
+        in_specs=[FAR] * 3 + [NEAR] + [FAR] * 3,
         out_specs=(FAR,) * 4,
         scratch_shapes=[
+            pltpu.SMEM((slots,), jnp.int32),
+            pltpu.SMEM((slots,), jnp.int32),
+            pltpu.SMEM((slots,), jnp.int32),
             pltpu.VMEM((experts * (height + 1), LANES), jnp.float32),
             pltpu.VMEM(master.shape, jnp.float32),
             pltpu.VMEM(one.shape, jnp.bfloat16),
             pltpu.VMEM(two.shape, jnp.bfloat16),
             pltpu.VMEM(pieces.shape, jnp.bfloat16),
+            pltpu.SemaphoreType.DMA((3,)),
             pltpu.SemaphoreType.DMA((3, tiles)),
             pltpu.SemaphoreType.DMA((3, tiles)),
             pltpu.SemaphoreType.DMA((sends,)),
@@ -312,7 +350,7 @@
         store(part).wait()
 
 
-def chunk_rows(arrived, hidden, width, parts=4, members=8):
+def chunk_rows(arrived, hidden, width, parts=8, members=8):
     slots, height, _ = arrived.shape
     blocks = width // LANES
     share = height // blocks
@@ -340,14 +378,9 @@
     devices = lax.axis_size("dev")
     experts, share, width = master.shape
     hidden = saved.shape[2]
-    row_count = saved.shape[1]
     chunks = slot_chunks(saved[0], cot_rows, live_rows, devices)
     received = exchange(chunks)
-    row_index = jnp.arange(row_count, dtype=jnp.int32)
-    masked = jnp.where(
-        (row_index < live_rows[0])[:, None], cot_rows, jnp.zeros_like(cot_rows)
-    )
-    input_grads = contract_cols(masked, weights[0]).astype(jnp.bfloat16)
+    input_grads = input_rows(cot_rows, weights[0], live_rows)
     slot_index = jnp.arange(devices, dtype=jnp.int32)
     bounds = jnp.cumsum(counts)
     holders = jnp.sum((bounds[None, :] <= slot_index[:, None]).astype(jnp.int32), axis=1)

time: 118 us -> 118 us (level)
  matrix products: 7.78 us -> 0 us
  Pallas kernels: 17.1 us -> 21.4 us
  local copies, waits for them, and re-layouts: 0.1 us -> 4.17 us
    dot_general x1 -> x0, matrix products: 7.78 us -> none  [contract_cols(): lax.dot_general(left, right, (((1,), (1,)), ((), ())), preferred_element_...]
    pallas_call x0 -> x1, Pallas kernels: none -> 4.82 us  [input_rows(): pl.pallas_call(inputs_kernel, out_shape=jax.ShapeDtypeStruct((rows, hidde...]
    unnamed x2 -> x6, local copies, waits for them, and re-layouts: 0.01 us -> 4.08 us
  transfers between devices with their start and end apart: 2 -> 2, of which waited for: 2 -> 2; matrix products, arithmetic and copies ran while one was open for 8% -> 1% of each run, Pallas kernels for 0% -> 4%
where the time goes in v2:
time: 118 us; the launch traced here: 117 us
  waiting for transfers between devices  72.8 us (62%)
  Pallas kernels  21.4 us (18%)
  starting transfers between devices  16.1 us (14%)
  local copies, waits for them, and re-layouts  4.17 us (4%)
  other arithmetic  1.5 us (1%)
  between operations  1.34 us (1%)
    all_to_all x2, waiting for transfers between devices, exchange(): lax.all_to_all(chunks, 'dev', split_axis=0, concat_axis=0, tiled=True)  72.8 us
    all_to_all x2, starting transfers between devices, exchange(): lax.all_to_all(chunks, 'dev', split_axis=0, concat_axis=0, tiled=True)  16.1 us
    pallas_call x1, Pallas kernels, slot_chunks(): pl.pallas_call(grads_kernel, out_shape=jax.ShapeDtypeStruct((devices, blo...  7.92 us
    pallas_call x1, Pallas kernels, adam_step(): pl.pallas_call(adam_kernel, out_shape=(pltpu.HBM(master.shape, jnp.float3...  6.58 us
    pallas_call x1, Pallas kernels, input_rows(): pl.pallas_call(inputs_kernel, out_shape=jax.ShapeDtypeStruct((rows, hidde...  4.82 us
    unnamed x6, local copies, waits for them, and re-layouts  4.08 us
  transfers between devices with their start and end apart: 2, of which 2 were waited for; matrix products, arithmetic and copies ran while one was open for 1% of the time, Pallas kernels for 4%

profile of v2, /device:TPU:1, one launch (start us, length us, event | category | flops | bytes accessed | tf_op | source)
XLA Modules:
  0.0 117.4 jit_solution(8187442173588075047)
XLA Ops:
  1.3 7.9 %slot_chunks.1 = bf16[128,96,128]{2,1,0:T(8,128)(2,1)} custom-call(s32[1]{0:T(128)S(6)} %copy.17.live_ref, bf16[1024,768]{1,0:T(8,128)(2,1)} %bitcast.21, bf16[1024,2048]{1,0:T(8,128)(2,1)} %bitcast.12), custom_call_target="tpu_custom_call" | custom-call | flops 3221225472 | bytes 8912896 | tf_op jit(solution)/shard_map/slot_chunks/pallas_call | solution.py:120
  9.2 0.0 copy-start.2
  9.2 11.5 %all-to-all-start = ((bf16[128,96,128]{2,1,0:T(8,128)(2,1)}), bf16[128,96,128]{2,1,0:T(8,128)(2,1)S(1)}, u32[]{:S(2)}, u32[]{:S(2)}) async-start(bf16[128,96,128]{2,1,0:T(8,128)(2,1)} %slot_chunks.1), calls=%async_computation | async-start | bytes 6291456 | tf_op jit(solution)/shard_map/all_to_all | solution.py:373
  20.7 0.0 copy-done.2
  20.7 0.1 copy.16
  20.8 0.1 reduce-window.8
  20.9 0.1 reduce
  21.0 0.1 fusion
  21.1 0.6 convert_reduce_fusion.holder_far
  21.7 0.6 or_convert_fusion.fresh_far
  22.3 40.0 %all-to-all-done.pieces = bf16[128,96,128]{2,1,0:T(8,128)(2,1)S(1)} async-done(((bf16[128,96,128]{2,1,0:T(8,128)(2,1)}), bf16[128,96,128]{2,1,0:T(8,128)(2,1)S(1)}, u32[]{:S(2)}, u32[]{:S(2)}) %all-to-all-start) | async-done | bytes 3145760 | tf_op jit(solution)/shard_map/all_to_all | solution.py:373
  62.3 6.6 %adam_step.1 = (f32[6,64,2048]{2,1,0:T(8,128)}, bf16[6,64,2048]{2,1,0:T(8,128)(2,1)}, bf16[6,64,2048]{2,1,0:T(8,128)(2,1)}, bf16[128,96,128]{2,1,0:T(8,128)(2,1)}) custom-call(s32[128]{0:T(128)} %convert_reduce_fusion.holder_far, s32[128]{0:T(128)} %or_convert_fusion.fresh_far, s32[128]{0:T(128)} %next_far.1, bf16[128,96,128]{2,1,0:T(8,128)(2,1)S(1)} %all-to-all-done.pieces, ...), custom_call_target="tpu_custom_call" | custom-call | tf_op jit(solution)/shard_map/adam_step/pallas_call | solution.py:286
  68.9 4.6 %all-to-all-start.1 = ((bf16[128,96,128]{2,1,0:T(8,128)(2,1)}), bf16[128,96,128]{2,1,0:T(8,128)(2,1)S(1)}, u32[]{:S(2)}, u32[]{:S(2)}) async-start(bf16[128,96,128]{2,1,0:T(8,128)(2,1)} %get-tuple-element.12), calls=%async_computation.1 | async-start | bytes 6291456 | tf_op jit(solution)/shard_map/all_to_all | solution.py:373
  73.5 0.0 copy-start
  73.6 2.2 %copy-done = bf16[1,1024,2048]{2,1,0:T(8,128)(2,1)S(1)} copy-done((bf16[1,1024,2048]{2,1,0:T(8,128)(2,1)S(1)}, bf16[1,1024,2048]{2,1,0:T(8,128)(2,1)}, u32[]{:S(2)}) %copy-start) | copy-done | bytes 4194328
  75.7 0.0 copy-start.1
  75.7 1.9 %copy-done.1 = bf16[1,768,2048]{2,1,0:T(8,128)(2,1)S(1)} copy-done((bf16[1,768,2048]{2,1,0:T(8,128)(2,1)S(1)}, bf16[1,768,2048]{2,1,0:T(8,128)(2,1)}, u32[]{:S(2)}) %copy-start.1) | copy-done | bytes 3145752
  77.6 4.8 %input_rows.1 = bf16[1024,768]{1,0:T(8,128)(2,1)} custom-call(s32[1]{0:T(128)S(6)} %copy.17.live_ref, bf16[1024,2048]{1,0:T(8,128)(2,1)S(1)} %bitcast.13, bf16[768,2048]{1,0:T(8,128)(2,1)S(1)} %bitcast.14), custom_call_target="tpu_custom_call" | custom-call | flops 3221225472 | bytes 8912896 | tf_op jit(solution)/shard_map/input_rows/pallas_call | solution.py:155
  82.5 32.8 %all-to-all-done.1.arrived = bf16[128,96,128]{2,1,0:T(8,128)(2,1)S(1)} async-done(((bf16[128,96,128]{2,1,0:T(8,128)(2,1)}), bf16[128,96,128]{2,1,0:T(8,128)(2,1)S(1)}, u32[]{:S(2)}, u32[]{:S(2)}) %all-to-all-start.1) | async-done | bytes 3145760 | tf_op jit(solution)/shard_map/all_to_all | solution.py:373
  115.3 2.1 %chunk_rows.1 = bf16[768,2048]{1,0:T(8,128)(2,1)} custom-call(bf16[128,96,128]{2,1,0:T(8,128)(2,1)S(1)} %all-to-all-done.1.arrived), custom_call_target="tpu_custom_call" | custom-call | tf_op jit(solution)/shard_map/chunk_rows/pallas_call | solution.py:357
Async XLA Ops:
  9.2 11.5 %copy-start.2 = (s32[64]{0:T(128)S(1)}, s32[64]{0:T(128)}, u32[]{:S(2)}) copy-start(s32[64]{0:T(128)} %param.12) | copy-start | bytes 772
  9.2 53.1 %all-to-all-start = ((bf16[128,96,128]{2,1,0:T(8,128)(2,1)}), bf16[128,96,128]{2,1,0:T(8,128)(2,1)S(1)}, u32[]{:S(2)}, u32[]{:S(2)}) async-start(bf16[128,96,128]{2,1,0:T(8,128)(2,1)} %slot_chunks.1), calls=%async_computation | async-start | bytes 6291456 | tf_op jit(solution)/shard_map/all_to_all | solution.py:373
  68.9 46.4 %all-to-all-start.1 = ((bf16[128,96,128]{2,1,0:T(8,128)(2,1)}), bf16[128,96,128]{2,1,0:T(8,128)(2,1)S(1)}, u32[]{:S(2)}, u32[]{:S(2)}) async-start(bf16[128,96,128]{2,1,0:T(8,128)(2,1)} %get-tuple-element.12), calls=%async_computation.1 | async-start | bytes 6291456 | tf_op jit(solution)/shard_map/all_to_all | solution.py:373
  73.5 2.2 %copy-start = (bf16[1,1024,2048]{2,1,0:T(8,128)(2,1)S(1)}, bf16[1,1024,2048]{2,1,0:T(8,128)(2,1)}, u32[]{:S(2)}) copy-start(bf16[1,1024,2048]{2,1,0:T(8,128)(2,1)} %param.10) | copy-start | bytes 12582916
  75.7 1.9 %copy-start.1 = (bf16[1,768,2048]{2,1,0:T(8,128)(2,1)S(1)}, bf16[1,768,2048]{2,1,0:T(8,128)(2,1)}, u32[]{:S(2)}) copy-start(bf16[1,768,2048]{2,1,0:T(8,128)(2,1)} %param.11) | copy-start | bytes 9437188

commit v3 on v2

--- a/solution.py
+++ b/solution.py
@@ -96,20 +96,28 @@
 
     @pl.loop(0, steps)
     def _(step):
+        before = lax.rem(step + steps - 1, steps)
+        for device in range(devices):
+            packed[before, device] = ordered[device].astype(jnp.bfloat16)
         multiply(step, ordered)
 
-        @pl.loop(0, devices // 8)
-        def _(eight):
-            for member in range(8):
-                packed[step, eight * 8 + member] = ordered[eight * 8 + member].astype(jnp.bfloat16)
-
-        send(step).start()
-
+        @pl.when(step > 0)
+        def _():
+            send(before).start()
+
+    @pl.loop(0, devices // 8)
+    def _(eight):
+        for member in range(8):
+            packed[steps - 1, eight * 8 + member] = ordered[eight * 8 + member].astype(
+                jnp.bfloat16
+            )
+
+    send(steps - 1).start()
     for step in range(steps):
         send(step).wait()
 
 
-def slot_chunks(saved, cot, live, devices, steps=4, bands=4):
+def slot_chunks(saved, cot, live, devices, steps=4, bands=2):
     rows, hidden = saved.shape
     width = cot.shape[1]
     thin = 2 * LANES

time: 118 us -> 118 us (level)
  no operation moved by 1% of the time
where the time goes in v3:
time: 118 us; the launch traced here: 117 us
  waiting for transfers between devices  72.8 us (62%)
  Pallas kernels  21.2 us (18%)
  starting transfers between devices  16.1 us (14%)
  local copies, waits for them, and re-layouts  4.17 us (4%)
  other arithmetic  1.5 us (1%)
  between operations  1.34 us (1%)
    all_to_all x2, waiting for transfers between devices, exchange(): lax.all_to_all(chunks, 'dev', split_axis=0, concat_axis=0, tiled=True)  72.8 us
    all_to_all x2, starting transfers between devices, exchange(): lax.all_to_all(chunks, 'dev', split_axis=0, concat_axis=0, tiled=True)  16.1 us
    pallas_call x1, Pallas kernels, slot_chunks(): pl.pallas_call(grads_kernel, out_shape=jax.ShapeDtypeStruct((devices, blo...  7.76 us
    pallas_call x1, Pallas kernels, adam_step(): pl.pallas_call(adam_kernel, out_shape=(pltpu.HBM(master.shape, jnp.float3...  6.58 us
    pallas_call x1, Pallas kernels, input_rows(): pl.pallas_call(inputs_kernel, out_shape=jax.ShapeDtypeStruct((rows, hidde...  4.82 us
    unnamed x6, local copies, waits for them, and re-layouts  4.08 us
  transfers between devices with their start and end apart: 2, of which 2 were waited for; matrix products, arithmetic and copies ran while one was open for 1% of the time, Pallas kernels for 4%

profile of v3, /device:TPU:1, one launch (start us, length us, event | category | flops | bytes accessed | tf_op | source)
XLA Modules:
  0.0 117.2 jit_solution(12427066976082767229)
XLA Ops:
  1.3 7.8 %slot_chunks.1 = bf16[128,96,128]{2,1,0:T(8,128)(2,1)} custom-call(s32[1]{0:T(128)S(6)} %copy.17.live_ref, bf16[1024,768]{1,0:T(8,128)(2,1)} %bitcast.21, bf16[1024,2048]{1,0:T(8,128)(2,1)} %bitcast.12), custom_call_target="tpu_custom_call" | custom-call | flops 3221225472 | bytes 8912896 | tf_op jit(solution)/shard_map/slot_chunks/pallas_call | solution.py:128
  9.0 0.0 copy-start.2
  9.1 11.5 %all-to-all-start = ((bf16[128,96,128]{2,1,0:T(8,128)(2,1)}), bf16[128,96,128]{2,1,0:T(8,128)(2,1)S(1)}, u32[]{:S(2)}, u32[]{:S(2)}) async-start(bf16[128,96,128]{2,1,0:T(8,128)(2,1)} %slot_chunks.1), calls=%async_computation | async-start | bytes 6291456 | tf_op jit(solution)/shard_map/all_to_all | solution.py:381
  20.6 0.0 copy-done.2
  20.6 0.1 copy.16
  20.7 0.1 reduce-window.8
  20.8 0.1 reduce
  20.9 0.1 fusion
  21.0 0.6 convert_reduce_fusion.holder_far
  21.6 0.6 or_convert_fusion.fresh_far
  22.2 40.0 %all-to-all-done.pieces = bf16[128,96,128]{2,1,0:T(8,128)(2,1)S(1)} async-done(((bf16[128,96,128]{2,1,0:T(8,128)(2,1)}), bf16[128,96,128]{2,1,0:T(8,128)(2,1)S(1)}, u32[]{:S(2)}, u32[]{:S(2)}) %all-to-all-start) | async-done | bytes 3145760 | tf_op jit(solution)/shard_map/all_to_all | solution.py:381
  62.1 6.6 %adam_step.1 = (f32[6,64,2048]{2,1,0:T(8,128)}, bf16[6,64,2048]{2,1,0:T(8,128)(2,1)}, bf16[6,64,2048]{2,1,0:T(8,128)(2,1)}, bf16[128,96,128]{2,1,0:T(8,128)(2,1)}) custom-call(s32[128]{0:T(128)} %convert_reduce_fusion.holder_far, s32[128]{0:T(128)} %or_convert_fusion.fresh_far, s32[128]{0:T(128)} %next_far.1, bf16[128,96,128]{2,1,0:T(8,128)(2,1)S(1)} %all-to-all-done.pieces, ...), custom_call_target="tpu_custom_call" | custom-call | tf_op jit(solution)/shard_map/adam_step/pallas_call | solution.py:294
  68.7 4.6 %all-to-all-start.1 = ((bf16[128,96,128]{2,1,0:T(8,128)(2,1)}), bf16[128,96,128]{2,1,0:T(8,128)(2,1)S(1)}, u32[]{:S(2)}, u32[]{:S(2)}) async-start(bf16[128,96,128]{2,1,0:T(8,128)(2,1)} %get-tuple-element.12), calls=%async_computation.1 | async-start | bytes 6291456 | tf_op jit(solution)/shard_map/all_to_all | solution.py:381
  73.4 0.0 copy-start
  73.4 2.2 %copy-done = bf16[1,1024,2048]{2,1,0:T(8,128)(2,1)S(1)} copy-done((bf16[1,1024,2048]{2,1,0:T(8,128)(2,1)S(1)}, bf16[1,1024,2048]{2,1,0:T(8,128)(2,1)}, u32[]{:S(2)}) %copy-start) | copy-done | bytes 4194328
  75.6 0.0 copy-start.1
  75.6 1.9 %copy-done.1 = bf16[1,768,2048]{2,1,0:T(8,128)(2,1)S(1)} copy-done((bf16[1,768,2048]{2,1,0:T(8,128)(2,1)S(1)}, bf16[1,768,2048]{2,1,0:T(8,128)(2,1)}, u32[]{:S(2)}) %copy-start.1) | copy-done | bytes 3145752
  77.5 4.8 %input_rows.1 = bf16[1024,768]{1,0:T(8,128)(2,1)} custom-call(s32[1]{0:T(128)S(6)} %copy.17.live_ref, bf16[1024,2048]{1,0:T(8,128)(2,1)S(1)} %bitcast.13, bf16[768,2048]{1,0:T(8,128)(2,1)S(1)} %bitcast.14), custom_call_target="tpu_custom_call" | custom-call | flops 3221225472 | bytes 8912896 | tf_op jit(solution)/shard_map/input_rows/pallas_call | solution.py:163
  82.3 32.8 %all-to-all-done.1.arrived = bf16[128,96,128]{2,1,0:T(8,128)(2,1)S(1)} async-done(((bf16[128,96,128]{2,1,0:T(8,128)(2,1)}), bf16[128,96,128]{2,1,0:T(8,128)(2,1)S(1)}, u32[]{:S(2)}, u32[]{:S(2)}) %all-to-all-start.1) | async-done | bytes 3145760 | tf_op jit(solution)/shard_map/all_to_all | solution.py:381
  115.1 2.1 %chunk_rows.1 = bf16[768,2048]{1,0:T(8,128)(2,1)} custom-call(bf16[128,96,128]{2,1,0:T(8,128)(2,1)S(1)} %all-to-all-done.1.arrived), custom_call_target="tpu_custom_call" | custom-call | tf_op jit(solution)/shard_map/chunk_rows/pallas_call | solution.py:365
Async XLA Ops:
  9.0 11.5 %copy-start.2 = (s32[64]{0:T(128)S(1)}, s32[64]{0:T(128)}, u32[]{:S(2)}) copy-start(s32[64]{0:T(128)} %param.12) | copy-start | bytes 772
  9.1 53.1 %all-to-all-start = ((bf16[128,96,128]{2,1,0:T(8,128)(2,1)}), bf16[128,96,128]{2,1,0:T(8,128)(2,1)S(1)}, u32[]{:S(2)}, u32[]{:S(2)}) async-start(bf16[128,96,128]{2,1,0:T(8,128)(2,1)} %slot_chunks.1), calls=%async_computation | async-start | bytes 6291456 | tf_op jit(solution)/shard_map/all_to_all | solution.py:381
  68.7 46.4 %all-to-all-start.1 = ((bf16[128,96,128]{2,1,0:T(8,128)(2,1)}), bf16[128,96,128]{2,1,0:T(8,128)(2,1)S(1)}, u32[]{:S(2)}, u32[]{:S(2)}) async-start(bf16[128,96,128]{2,1,0:T(8,128)(2,1)} %get-tuple-element.12), calls=%async_computation.1 | async-start | bytes 6291456 | tf_op jit(solution)/shard_map/all_to_all | solution.py:381
  73.4 2.2 %copy-start = (bf16[1,1024,2048]{2,1,0:T(8,128)(2,1)S(1)}, bf16[1,1024,2048]{2,1,0:T(8,128)(2,1)}, u32[]{:S(2)}) copy-start(bf16[1,1024,2048]{2,1,0:T(8,128)(2,1)} %param.10) | copy-start | bytes 12582916
  75.6 1.9 %copy-start.1 = (bf16[1,768,2048]{2,1,0:T(8,128)(2,1)S(1)}, bf16[1,768,2048]{2,1,0:T(8,128)(2,1)}, u32[]{:S(2)}) copy-start(bf16[1,768,2048]{2,1,0:T(8,128)(2,1)} %param.11) | copy-start | bytes 9437188

commit v4 on v3

--- a/solution.py
+++ b/solution.py
@@ -74,16 +74,13 @@
 
     for band in range(bands):
         load_saved(band).start()
+    for strip in range(per_step):
+        load_cot(strip).start()
 
     @pl.loop(0, bands)
     def _(band):
         span = pl.ds(pl.multiple_of(band * band_rows, band_rows), band_rows)
         pltpu.make_async_copy(saved_ref.at[span], saved_in.at[span], saved_sem.at[band]).wait()
-
-        @pl.when(band == 0)
-        def _():
-            for strip in range(per_step):
-                load_cot(strip).start()
 
         index = lax.broadcasted_iota(jnp.int32, (band_rows, hidden), 0)
         part = saved_in[span, :]

time: 118 us -> 117 us (level)
  no operation moved by 1% of the time
where the time goes in v4:
time: 117 us
  waiting for transfers between devices  72.8 us (62%)
  Pallas kernels  20.8 us (18%)
  starting transfers between devices  16.1 us (14%)
  local copies, waits for them, and re-layouts  4.17 us (4%)
  other arithmetic  1.5 us (1%)
  between operations  1.34 us (1%)
    all_to_all x2, waiting for transfers between devices, exchange(): lax.all_to_all(chunks, 'dev', split_axis=0, concat_axis=0, tiled=True)  72.8 us
    all_to_all x2, starting transfers between devices, exchange(): lax.all_to_all(chunks, 'dev', split_axis=0, concat_axis=0, tiled=True)  16.1 us
    pallas_call x1, Pallas kernels, slot_chunks(): pl.pallas_call(grads_kernel, out_shape=jax.ShapeDtypeStruct((devices, blo...  7.26 us
    pallas_call x1, Pallas kernels, adam_step(): pl.pallas_call(adam_kernel, out_shape=(pltpu.HBM(master.shape, jnp.float3...  6.58 us
    pallas_call x1, Pallas kernels, input_rows(): pl.pallas_call(inputs_kernel, out_shape=jax.ShapeDtypeStruct((rows, hidde...  4.82 us
    unnamed x6, local copies, waits for them, and re-layouts  4.08 us
  transfers between devices with their start and end apart: 2, of which 2 were waited for; matrix products, arithmetic and copies ran while one was open for 1% of the time, Pallas kernels for 4%

profile of v4, /device:TPU:1, one launch (start us, length us, event | category | flops | bytes accessed | tf_op | source)
XLA Modules:
  0.0 116.7 jit_solution(13936695050822163174)
XLA Ops:
  1.3 7.3 %slot_chunks.1 = bf16[128,96,128]{2,1,0:T(8,128)(2,1)} custom-call(s32[1]{0:T(128)S(6)} %copy.17.live_ref, bf16[1024,768]{1,0:T(8,128)(2,1)} %bitcast.21, bf16[1024,2048]{1,0:T(8,128)(2,1)} %bitcast.12), custom_call_target="tpu_custom_call" | custom-call | flops 3221225472 | bytes 8912896 | tf_op jit(solution)/shard_map/slot_chunks/pallas_call | solution.py:125
  8.5 0.0 copy-start.2
  8.6 11.5 %all-to-all-start = ((bf16[128,96,128]{2,1,0:T(8,128)(2,1)}), bf16[128,96,128]{2,1,0:T(8,128)(2,1)S(1)}, u32[]{:S(2)}, u32[]{:S(2)}) async-start(bf16[128,96,128]{2,1,0:T(8,128)(2,1)} %slot_chunks.1), calls=%async_computation | async-start | bytes 6291456 | tf_op jit(solution)/shard_map/all_to_all | solution.py:378
  20.1 0.0 copy-done.2
  20.1 0.1 copy.16
  20.2 0.1 reduce-window.8
  20.3 0.1 reduce
  20.4 0.1 fusion
  20.5 0.6 convert_reduce_fusion.holder_far
  21.1 0.6 or_convert_fusion.fresh_far
  21.7 40.0 %all-to-all-done.pieces = bf16[128,96,128]{2,1,0:T(8,128)(2,1)S(1)} async-done(((bf16[128,96,128]{2,1,0:T(8,128)(2,1)}), bf16[128,96,128]{2,1,0:T(8,128)(2,1)S(1)}, u32[]{:S(2)}, u32[]{:S(2)}) %all-to-all-start) | async-done | bytes 3145760 | tf_op jit(solution)/shard_map/all_to_all | solution.py:378
  61.7 6.6 %adam_step.1 = (f32[6,64,2048]{2,1,0:T(8,128)}, bf16[6,64,2048]{2,1,0:T(8,128)(2,1)}, bf16[6,64,2048]{2,1,0:T(8,128)(2,1)}, bf16[128,96,128]{2,1,0:T(8,128)(2,1)}) custom-call(s32[128]{0:T(128)} %convert_reduce_fusion.holder_far, s32[128]{0:T(128)} %or_convert_fusion.fresh_far, s32[128]{0:T(128)} %next_far.1, bf16[128,96,128]{2,1,0:T(8,128)(2,1)S(1)} %all-to-all-done.pieces, ...), custom_call_target="tpu_custom_call" | custom-call | tf_op jit(solution)/shard_map/adam_step/pallas_call | solution.py:291
  68.2 4.6 %all-to-all-start.1 = ((bf16[128,96,128]{2,1,0:T(8,128)(2,1)}), bf16[128,96,128]{2,1,0:T(8,128)(2,1)S(1)}, u32[]{:S(2)}, u32[]{:S(2)}) async-start(bf16[128,96,128]{2,1,0:T(8,128)(2,1)} %get-tuple-element.12), calls=%async_computation.1 | async-start | bytes 6291456 | tf_op jit(solution)/shard_map/all_to_all | solution.py:378
  72.9 0.0 copy-start
  72.9 2.2 %copy-done = bf16[1,1024,2048]{2,1,0:T(8,128)(2,1)S(1)} copy-done((bf16[1,1024,2048]{2,1,0:T(8,128)(2,1)S(1)}, bf16[1,1024,2048]{2,1,0:T(8,128)(2,1)}, u32[]{:S(2)}) %copy-start) | copy-done | bytes 4194328
  75.1 0.0 copy-start.1
  75.1 1.9 %copy-done.1 = bf16[1,768,2048]{2,1,0:T(8,128)(2,1)S(1)} copy-done((bf16[1,768,2048]{2,1,0:T(8,128)(2,1)S(1)}, bf16[1,768,2048]{2,1,0:T(8,128)(2,1)}, u32[]{:S(2)}) %copy-start.1) | copy-done | bytes 3145752
  77.0 4.8 %input_rows.1 = bf16[1024,768]{1,0:T(8,128)(2,1)} custom-call(s32[1]{0:T(128)S(6)} %copy.17.live_ref, bf16[1024,2048]{1,0:T(8,128)(2,1)S(1)} %bitcast.13, bf16[768,2048]{1,0:T(8,128)(2,1)S(1)} %bitcast.14), custom_call_target="tpu_custom_call" | custom-call | flops 3221225472 | bytes 8912896 | tf_op jit(solution)/shard_map/input_rows/pallas_call | solution.py:160
  81.8 32.8 %all-to-all-done.1.arrived = bf16[128,96,128]{2,1,0:T(8,128)(2,1)S(1)} async-done(((bf16[128,96,128]{2,1,0:T(8,128)(2,1)}), bf16[128,96,128]{2,1,0:T(8,128)(2,1)S(1)}, u32[]{:S(2)}, u32[]{:S(2)}) %all-to-all-start.1) | async-done | bytes 3145760 | tf_op jit(solution)/shard_map/all_to_all | solution.py:378
  114.6 2.1 %chunk_rows.1 = bf16[768,2048]{1,0:T(8,128)(2,1)} custom-call(bf16[128,96,128]{2,1,0:T(8,128)(2,1)S(1)} %all-to-all-done.1.arrived), custom_call_target="tpu_custom_call" | custom-call | tf_op jit(solution)/shard_map/chunk_rows/pallas_call | solution.py:362
Async XLA Ops:
  8.5 11.5 %copy-start.2 = (s32[64]{0:T(128)S(1)}, s32[64]{0:T(128)}, u32[]{:S(2)}) copy-start(s32[64]{0:T(128)} %param.12) | copy-start | bytes 772
  8.6 53.1 %all-to-all-start = ((bf16[128,96,128]{2,1,0:T(8,128)(2,1)}), bf16[128,96,128]{2,1,0:T(8,128)(2,1)S(1)}, u32[]{:S(2)}, u32[]{:S(2)}) async-start(bf16[128,96,128]{2,1,0:T(8,128)(2,1)} %slot_chunks.1), calls=%async_computation | async-start | bytes 6291456 | tf_op jit(solution)/shard_map/all_to_all | solution.py:378
  68.2 46.4 %all-to-all-start.1 = ((bf16[128,96,128]{2,1,0:T(8,128)(2,1)}), bf16[128,96,128]{2,1,0:T(8,128)(2,1)S(1)}, u32[]{:S(2)}, u32[]{:S(2)}) async-start(bf16[128,96,128]{2,1,0:T(8,128)(2,1)} %get-tuple-element.12), calls=%async_computation.1 | async-start | bytes 6291456 | tf_op jit(solution)/shard_map/all_to_all | solution.py:378
  72.9 2.2 %copy-start = (bf16[1,1024,2048]{2,1,0:T(8,128)(2,1)S(1)}, bf16[1,1024,2048]{2,1,0:T(8,128)(2,1)}, u32[]{:S(2)}) copy-start(bf16[1,1024,2048]{2,1,0:T(8,128)(2,1)} %param.10) | copy-start | bytes 12582916
  75.1 1.9 %copy-start.1 = (bf16[1,768,2048]{2,1,0:T(8,128)(2,1)S(1)}, bf16[1,768,2048]{2,1,0:T(8,128)(2,1)}, u32[]{:S(2)}) copy-start(bf16[1,768,2048]{2,1,0:T(8,128)(2,1)} %param.11) | copy-start | bytes 9437188

commit v5 on v4

--- a/solution.py
+++ b/solution.py
@@ -114,7 +114,7 @@
         send(step).wait()
 
 
-def slot_chunks(saved, cot, live, devices, steps=4, bands=2):
+def slot_chunks(saved, cot, live, devices, steps=4, bands=4):
     rows, hidden = saved.shape
     width = cot.shape[1]
     thin = 2 * LANES

time: 117 us -> 117 us (level)
  no operation moved by 1% of the time
where the time goes in v5:
time: 117 us
  waiting for transfers between devices  72.8 us (62%)
  Pallas kernels  20.6 us (18%)
  starting transfers between devices  16.1 us (14%)
  local copies, waits for them, and re-layouts  4.17 us (4%)
  other arithmetic  1.5 us (1%)
  between operations  1.34 us (1%)
    all_to_all x2, waiting for transfers between devices, exchange(): lax.all_to_all(chunks, 'dev', split_axis=0, concat_axis=0, tiled=True)  72.8 us
    all_to_all x2, starting transfers between devices, exchange(): lax.all_to_all(chunks, 'dev', split_axis=0, concat_axis=0, tiled=True)  16.1 us
    pallas_call x1, Pallas kernels, slot_chunks(): pl.pallas_call(grads_kernel, out_shape=jax.ShapeDtypeStruct((devices, blo...  7.15 us
    pallas_call x1, Pallas kernels, adam_step(): pl.pallas_call(adam_kernel, out_shape=(pltpu.HBM(master.shape, jnp.float3...  6.58 us
    pallas_call x1, Pallas kernels, input_rows(): pl.pallas_call(inputs_kernel, out_shape=jax.ShapeDtypeStruct((rows, hidde...  4.82 us
    unnamed x6, local copies, waits for them, and re-layouts  4.08 us
  transfers between devices with their start and end apart: 2, of which 2 were waited for; matrix products, arithmetic and copies ran while one was open for 1% of the time, Pallas kernels for 4%

profile of v5, /device:TPU:1, one launch (start us, length us, event | category | flops | bytes accessed | tf_op | source)
XLA Modules:
  0.0 116.6 jit_solution(15115676693183646847)
XLA Ops:
  1.3 7.1 %slot_chunks.1 = bf16[128,96,128]{2,1,0:T(8,128)(2,1)} custom-call(s32[1]{0:T(128)S(6)} %copy.17.live_ref, bf16[1024,768]{1,0:T(8,128)(2,1)} %bitcast.21, bf16[1024,2048]{1,0:T(8,128)(2,1)} %bitcast.12), custom_call_target="tpu_custom_call" | custom-call | flops 3221225472 | bytes 8912896 | tf_op jit(solution)/shard_map/slot_chunks/pallas_call | solution.py:125
  8.4 0.0 copy-start.2
  8.4 11.5 %all-to-all-start = ((bf16[128,96,128]{2,1,0:T(8,128)(2,1)}), bf16[128,96,128]{2,1,0:T(8,128)(2,1)S(1)}, u32[]{:S(2)}, u32[]{:S(2)}) async-start(bf16[128,96,128]{2,1,0:T(8,128)(2,1)} %slot_chunks.1), calls=%async_computation | async-start | bytes 6291456 | tf_op jit(solution)/shard_map/all_to_all | solution.py:378
  19.9 0.0 copy-done.2
  20.0 0.1 copy.16
  20.1 0.1 reduce-window.8
  20.1 0.1 reduce
  20.3 0.1 fusion
  20.4 0.6 convert_reduce_fusion.holder_far
  21.0 0.6 or_convert_fusion.fresh_far
  21.6 40.0 %all-to-all-done.pieces = bf16[128,96,128]{2,1,0:T(8,128)(2,1)S(1)} async-done(((bf16[128,96,128]{2,1,0:T(8,128)(2,1)}), bf16[128,96,128]{2,1,0:T(8,128)(2,1)S(1)}, u32[]{:S(2)}, u32[]{:S(2)}) %all-to-all-start) | async-done | bytes 3145760 | tf_op jit(solution)/shard_map/all_to_all | solution.py:378
  61.5 6.6 %adam_step.1 = (f32[6,64,2048]{2,1,0:T(8,128)}, bf16[6,64,2048]{2,1,0:T(8,128)(2,1)}, bf16[6,64,2048]{2,1,0:T(8,128)(2,1)}, bf16[128,96,128]{2,1,0:T(8,128)(2,1)}) custom-call(s32[128]{0:T(128)} %convert_reduce_fusion.holder_far, s32[128]{0:T(128)} %or_convert_fusion.fresh_far, s32[128]{0:T(128)} %next_far.1, bf16[128,96,128]{2,1,0:T(8,128)(2,1)S(1)} %all-to-all-done.pieces, ...), custom_call_target="tpu_custom_call" | custom-call | tf_op jit(solution)/shard_map/adam_step/pallas_call | solution.py:291
  68.1 4.6 %all-to-all-start.1 = ((bf16[128,96,128]{2,1,0:T(8,128)(2,1)}), bf16[128,96,128]{2,1,0:T(8,128)(2,1)S(1)}, u32[]{:S(2)}, u32[]{:S(2)}) async-start(bf16[128,96,128]{2,1,0:T(8,128)(2,1)} %get-tuple-element.12), calls=%async_computation.1 | async-start | bytes 6291456 | tf_op jit(solution)/shard_map/all_to_all | solution.py:378
  72.8 0.0 copy-start
  72.8 2.2 %copy-done = bf16[1,1024,2048]{2,1,0:T(8,128)(2,1)S(1)} copy-done((bf16[1,1024,2048]{2,1,0:T(8,128)(2,1)S(1)}, bf16[1,1024,2048]{2,1,0:T(8,128)(2,1)}, u32[]{:S(2)}) %copy-start) | copy-done | bytes 4194328
  75.0 0.0 copy-start.1
  75.0 1.9 %copy-done.1 = bf16[1,768,2048]{2,1,0:T(8,128)(2,1)S(1)} copy-done((bf16[1,768,2048]{2,1,0:T(8,128)(2,1)S(1)}, bf16[1,768,2048]{2,1,0:T(8,128)(2,1)}, u32[]{:S(2)}) %copy-start.1) | copy-done | bytes 3145752
  76.9 4.8 %input_rows.1 = bf16[1024,768]{1,0:T(8,128)(2,1)} custom-call(s32[1]{0:T(128)S(6)} %copy.17.live_ref, bf16[1024,2048]{1,0:T(8,128)(2,1)S(1)} %bitcast.13, bf16[768,2048]{1,0:T(8,128)(2,1)S(1)} %bitcast.14), custom_call_target="tpu_custom_call" | custom-call | flops 3221225472 | bytes 8912896 | tf_op jit(solution)/shard_map/input_rows/pallas_call | solution.py:160
  81.7 32.8 %all-to-all-done.1.arrived = bf16[128,96,128]{2,1,0:T(8,128)(2,1)S(1)} async-done(((bf16[128,96,128]{2,1,0:T(8,128)(2,1)}), bf16[128,96,128]{2,1,0:T(8,128)(2,1)S(1)}, u32[]{:S(2)}, u32[]{:S(2)}) %all-to-all-start.1) | async-done | bytes 3145760 | tf_op jit(solution)/shard_map/all_to_all | solution.py:378
  114.5 2.1 %chunk_rows.1 = bf16[768,2048]{1,0:T(8,128)(2,1)} custom-call(bf16[128,96,128]{2,1,0:T(8,128)(2,1)S(1)} %all-to-all-done.1.arrived), custom_call_target="tpu_custom_call" | custom-call | tf_op jit(solution)/shard_map/chunk_rows/pallas_call | solution.py:362
Async XLA Ops:
  8.4 11.5 %copy-start.2 = (s32[64]{0:T(128)S(1)}, s32[64]{0:T(128)}, u32[]{:S(2)}) copy-start(s32[64]{0:T(128)} %param.12) | copy-start | bytes 772
  8.4 53.1 %all-to-all-start = ((bf16[128,96,128]{2,1,0:T(8,128)(2,1)}), bf16[128,96,128]{2,1,0:T(8,128)(2,1)S(1)}, u32[]{:S(2)}, u32[]{:S(2)}) async-start(bf16[128,96,128]{2,1,0:T(8,128)(2,1)} %slot_chunks.1), calls=%async_computation | async-start | bytes 6291456 | tf_op jit(solution)/shard_map/all_to_all | solution.py:378
  68.1 46.4 %all-to-all-start.1 = ((bf16[128,96,128]{2,1,0:T(8,128)(2,1)}), bf16[128,96,128]{2,1,0:T(8,128)(2,1)S(1)}, u32[]{:S(2)}, u32[]{:S(2)}) async-start(bf16[128,96,128]{2,1,0:T(8,128)(2,1)} %get-tuple-element.12), calls=%async_computation.1 | async-start | bytes 6291456 | tf_op jit(solution)/shard_map/all_to_all | solution.py:378
  72.8 2.2 %copy-start = (bf16[1,1024,2048]{2,1,0:T(8,128)(2,1)S(1)}, bf16[1,1024,2048]{2,1,0:T(8,128)(2,1)}, u32[]{:S(2)}) copy-start(bf16[1,1024,2048]{2,1,0:T(8,128)(2,1)} %param.10) | copy-start | bytes 12582916
  75.0 1.9 %copy-start.1 = (bf16[1,768,2048]{2,1,0:T(8,128)(2,1)S(1)}, bf16[1,768,2048]{2,1,0:T(8,128)(2,1)}, u32[]{:S(2)}) copy-start(bf16[1,768,2048]{2,1,0:T(8,128)(2,1)} %param.11) | copy-start | bytes 9437188
